TPU v7x, 256 devices: a whole 4x4x8 slice. The times are simulated.
256 devices in a mesh: tm: 64 (over z, y, x_hi), chan: 4 (over x_lo, core).
Axes of the slice: x: 4 (x_hi: 2, x_lo: 2; x = x_hi * 2 + x_lo), y: 4, z: 8, core: 2. Of those that a mesh axis runs over, the one named last changes fastest.
Arguments:
- signal: bfloat16 [384, 8192], P('chan', 'tm'), may hold values from -6 to 6
- codes_init: float32 [128, 8192], P(None, 'tm'), may hold values from -2 to 2
- dictionary_init: float32 [128, 36864], P(None, 'chan'), may hold values from -6 to 6
- threshold: float32 [128], replicated, may hold values from 0.05 to 0.5
- plan: int32 [8], replicated, may hold values from 0 to 7, each once
Outputs:
- sparse_codes: float32 [128, 8192], P(None, 'tm')
- dictionary: float32 [128, 36864], P(None, 'chan')
- residual: float32 [384, 8192], P('chan', 'tm')
Inputs may be any that keep to these rules, and one draw needn't show every extreme that they name: `plan`: every atom block from 0 to 7 appears exactly once.
All inputs are finite; a program needn't handle non-finite values.
Results may differ from a plain program's by a relative error of at most 0.013.
Values may be sent and summed in bfloat16 or wider, within the bound.
A program may use at most 64 MiB of HBM per device.

v0:
```python
import jax
import jax.numpy as jnp
from jax import lax
from jax.sharding import PartitionSpec as P

C = 384
K = 128
L = 96
BLOCK_ATOMS = 16
INNER = 2
OUTER = 2
code_rate = 0.3
move_rate = 0.5
tiny_eps = 1e-06


def shifted(shard, axis, by):
    peers = lax.axis_size(axis)
    pairs = [(i, i + by) for i in range(peers) if 0 <= i + by < peers]
    return lax.ppermute(shard, axis, pairs)


def renew_atoms(old_atoms, across, mean_sq, spread):
    return (old_atoms + move_rate * across / jnp.sqrt(spread)[:, None]) / jnp.sqrt(mean_sq + 0.25)[
        :, None
    ]


def shards(signal, codes_init, dictionary_init, threshold, plan):
    segment = signal.shape[1]
    local_chan = signal.shape[0]
    unit_scale = (C * L) ** (-0.5)
    entries = C * L
    limit = threshold[:, None]

    def convolve(atom_cube, code_low):
        code_edge = shifted(code_low[:, segment - (L - 1) :], "tm", 1)
        extended = jnp.concatenate([code_edge, code_low], axis=1)
        lagged = jnp.stack(
            [extended[:, L - 1 - offset : L - 1 - offset + segment] for offset in range(L)], axis=1
        )
        return unit_scale * jnp.einsum(
            "kcl,klt->ct", atom_cube, lagged, preferred_element_type=jnp.float32
        )

    def resid_columns(resid_low):
        resid_edge = shifted(resid_low[:, : L - 1], "tm", -1)
        extended = jnp.concatenate([resid_low, resid_edge], axis=1)
        lagged = jnp.stack([extended[:, offset : offset + segment] for offset in range(L)], axis=1)
        return lagged.reshape(local_chan * L, segment)

    code_state = codes_init
    dictionary = dictionary_init
    residual = signal.astype(jnp.float32)
    for outer_step in range(OUTER):
        dict_low = dictionary.astype(jnp.bfloat16)
        atom_cube = dict_low.reshape(K, local_chan, L)
        for inner_step in range(INNER):
            code_low = code_state.astype(jnp.bfloat16)
            residual = signal.astype(jnp.float32) - convolve(atom_cube, code_low)
            lagged = resid_columns(residual.astype(jnp.bfloat16))
            partial_value = unit_scale * jnp.dot(
                dict_low, lagged, preferred_element_type=jnp.float32
            )
            scores = lax.psum(partial_value.astype(jnp.bfloat16), "chan").astype(jnp.float32)
            stepped = code_state + code_rate * scores
            code_state = stepped - jnp.clip(stepped, -limit, limit)
        code_low = code_state.astype(jnp.bfloat16)
        residual = signal.astype(jnp.float32) - convolve(atom_cube, code_low)
        lagged = resid_columns(residual.astype(jnp.bfloat16))
        first_row = plan[outer_step] * BLOCK_ATOMS
        code_block = lax.dynamic_slice_in_dim(code_low, first_row, BLOCK_ATOMS, 0)
        local_grad = lax.dot_general(
            code_block, lagged, (((1,), (1,)), ((), ())), preferred_element_type=jnp.float32
        )
        old_atoms = lax.dynamic_slice_in_dim(dictionary, first_row, BLOCK_ATOMS, 0)
        gradient = lax.psum(local_grad, "tm")
        dot_sum, square_sum = lax.psum(
            (jnp.sum(gradient * old_atoms, axis=1), jnp.sum(old_atoms * old_atoms, axis=1)), "chan"
        )
        mean_sq = square_sum / entries + tiny_eps
        along_coef = dot_sum / entries / mean_sq
        across = gradient - along_coef[:, None] * old_atoms
        spread = lax.psum(jnp.sum(across * across, axis=1), "chan") / entries + tiny_eps
        renewed = renew_atoms(old_atoms, across, mean_sq, spread)
        dictionary = lax.dynamic_update_slice_in_dim(dictionary, renewed, first_row, 0)
    return (code_state, dictionary, residual)


def solution(mesh):
    placed = (P("chan", "tm"), P(None, "tm"), P(None, "chan"), P(), P())
    return jax.shard_map(
        shards,
        mesh=mesh,
        in_specs=placed,
        out_specs=(P(None, "tm"), P(None, "chan"), P("chan", "tm")),
        check_vma=False,
    )
```

profile of v0, /device:TPU:1, one launch (start us, length us, event | category | flops | bytes accessed | tf_op | source)
XLA Modules:
  0.0 1790.4 jit_solution(17106135282890277592)
XLA Ops:
  7.2 5.0 copy.1188
  12.9 5.5 collective-permute-start
  18.4 3.6 copy.27
  87.9 3.6 constant_dynamic-update-slice_fusion.191
  92.9 4.7 collective-permute-done.1
  163.2 2.6 copy.29
  166.6 11.6 psum.84
  178.2 5.0 collective-permute-start.2
  188.6 5.1 collective-permute-done.3
  204.9 11.8 psum.85
  216.8 6.6 collective-permute-start.4
  231.1 3.6 collective-permute-done.5
  300.3 2.6 copy.40
  304.6 640.8 %all-reduce.5.cloned.1.call-done = f32[16,9216]{1,0:T(8,128)} async-done(((f32[16,9216]{1,0:T(8,128)}), f32[16,9216]{1,0:T(8,128)}) %all-reduce.5.cloned.1.call-update) | async-done | bytes 589840 | tf_op jit(solution)/shard_map/psum | solution.py:77
  946.9 36.4 %all-reduce.1 = (f32[16]{0:T(128)S(1)}, f32[16]{0:T(128)S(1)}) all-reduce(f32[16]{0:T(128)S(1)} %get-tuple-element.12, f32[16]{0:T(128)S(1)} %get-tuple-element.11), channel_id=1, replica_groups=mesh['tm'=64,'chan'=4] {'chan'}, use_global_device_ids=true, to_apply=%region_6.7 | all-reduce | flops 32 | bytes 256 | tf_op jit(solution)/shard_map/psum | solution.py:78
  984.8 5.9 psum.89
  990.7 2.1 divide_dynamic-update-slice_fusion.1
  992.8 2.6 convert_element_type.92
  995.4 2.4 copy.41
  997.9 3.6 constant_dynamic-update-slice_fusion.671
  1001.5 1.7 collective-permute-start.6
  1003.2 4.4 collective-permute-done.6
  1018.9 11.4 psum.90
  1030.3 5.8 collective-permute-start.7
  1042.3 4.9 collective-permute-done.8
  1058.5 12.3 psum.91
  1070.9 6.0 collective-permute-start.9
  1084.4 4.2 collective-permute-done.10
  1101.2 634.7 %all-reduce.7.cloned.1.call-done = f32[16,9216]{1,0:T(8,128)} async-done(((f32[16,9216]{1,0:T(8,128)}), f32[16,9216]{1,0:T(8,128)}) %all-reduce.7.cloned.1.call-update) | async-done | bytes 589840 | tf_op jit(solution)/shard_map/psum | solution.py:77
  1737.4 36.4 %all-reduce = (f32[16]{0:T(128)S(1)}, f32[16]{0:T(128)S(1)}) all-reduce(f32[16]{0:T(128)S(1)} %get-tuple-element.10, f32[16]{0:T(128)S(1)} %get-tuple-element.9), channel_id=1, replica_groups=mesh['tm'=64,'chan'=4] {'chan'}, use_global_device_ids=true, to_apply=%region_15.16 | all-reduce | flops 32 | bytes 256 | tf_op jit(solution)/shard_map/psum | solution.py:78
  1775.4 5.9 psum.95
  1781.3 2.1 divide_dynamic-update-slice_fusion
  (1115 shorter events, 277.1 us)
Async XLA Ops:
  7.2 5.0 copy-start.6
  7.2 938.2 %all-reduce.5.cloned.1.call-start = ((), (), s32[]{:S(2)}) async-start(), calls=%async_computation | async-start | bytes 1179648 | tf_op jit(solution)/shard_map/psum | solution.py:77
  12.9 9.1 collective-permute-start
  54.6 33.3 %copy-start.5 = (bf16[96,128]{1,0:T(8,128)(2,1)S(1)}, bf16[96,128]{1,0:T(8,128)(2,1)}, u32[]{:S(2)}) copy-start(bf16[96,128]{1,0:T(8,128)(2,1)} %param.5) | copy-start | bytes 73732
  87.9 5.0 copy-start.7
  91.5 6.1 collective-permute-start.1
  178.2 5.8 collective-permute-start.2
  187.3 6.4 collective-permute-start.3
  216.8 7.5 collective-permute-start.4
  226.7 1.7 copy-start.4
  226.7 3.2 copy-start.8
  228.4 6.3 collective-permute-start.5
  304.5 1431.4 %all-reduce.7.cloned.1.call-start = ((), (), s32[]{:S(2)}) async-start(), calls=%async_computation.1 | async-start | bytes 1179648 | tf_op jit(solution)/shard_map/psum | solution.py:77
  945.4 45.4 %copy-start.3 = (f32[16,9216]{1,0:T(8,128)S(1)}, f32[16,9216]{1,0:T(8,128)}, u32[]{:S(2)}) copy-start(f32[16,9216]{1,0:T(8,128)} %all-reduce.5.cloned.1.call-done) | copy-start | bytes 1769476
  1001.5 6.1 collective-permute-start.6
  1030.3 6.8 collective-permute-start.7
  1038.2 1.7 copy-start
  1040.8 6.4 collective-permute-start.8
  1070.9 7.0 collective-permute-start.9
  1079.0 1.7 copy-start.1
  1082.2 6.3 collective-permute-start.10
  1735.9 45.4 %copy-start.2 = (f32[16,9216]{1,0:T(8,128)S(1)}, f32[16,9216]{1,0:T(8,128)}, u32[]{:S(2)}) copy-start(f32[16,9216]{1,0:T(8,128)} %all-reduce.7.cloned.1.call-done) | copy-start | bytes 1769476
Sparse Core Ops, SparseCore 0:
  304.7 640.6 all-reduce.4
  1100.6 635.2 all-reduce.6
where the time goes:
time: 1800 us; the launch traced here: 1790 us
  waiting for transfers between devices  1310 us (73%)
  other arithmetic  255 us (14%)
  blocking collectives  132 us (7%)
  starting transfers between devices  37.7 us (2%)
  local copies, waits for them, and re-layouts  22.3 us (1%)
  matrix products  19.5 us (1%)
  between operations  18.7 us (1%)
    psum x2, waiting for transfers between devices, shards(): gradient = lax.psum(local_grad, 'tm')  1280 us
    unnamed x1039, other arithmetic  239 us
    psum x2, blocking collectives, shards(): lax.psum((jnp.sum(gradient * old_atoms, axis=1), jnp.sum(old_atoms * old_...  72.9 us
    psum x4, blocking collectives, shards(): lax.psum(partial_value.astype(jnp.bfloat16), 'chan').astype(jnp.float32)  47 us
    ppermute x11, starting transfers between devices, shifted(): return lax.ppermute(shard, axis, pairs)  37.6 us
  transfers between devices with their start and end apart: 13, of which 12 were waited for; matrix products, arithmetic and copies ran while one was open for 0% of the time, Pallas kernels for 0%

commit v1 on v0

--- a/solution.py
+++ b/solution.py
@@ -74,7 +74,7 @@
             code_block, lagged, (((1,), (1,)), ((), ())), preferred_element_type=jnp.float32
         )
         old_atoms = lax.dynamic_slice_in_dim(dictionary, first_row, BLOCK_ATOMS, 0)
-        gradient = lax.psum(local_grad, "tm")
+        gradient = jnp.sum(lax.all_gather(local_grad, "tm"), axis=0)
         dot_sum, square_sum = lax.psum(
             (jnp.sum(gradient * old_atoms, axis=1), jnp.sum(old_atoms * old_atoms, axis=1)), "chan"
         )

time: 1800 us -> 1260 us (0.70)
  waiting for transfers between devices: 1310 us -> 801 us
  blocking collectives: 132 us -> 71.8 us
  other arithmetic: 255 us -> 280 us
    psum x2 -> x0, waiting for transfers between devices: 1280 us -> none  [shards(): gradient = lax.psum(local_grad, 'tm')]
    all_gather x0 -> x2, waiting for transfers between devices: none -> 771 us  [shards(): gradient = jnp.sum(lax.all_gather(local_grad, 'tm'), axis=0)]
    psum x2, blocking collectives: 72.9 us -> 12.8 us  [shards(): lax.psum((jnp.sum(gradient * old_atoms, axis=1), jnp.sum(old_atoms * old_...]
    reduce_sum x0 -> x2, other arithmetic: none -> 26.3 us  [shards(): gradient = jnp.sum(lax.all_gather(local_grad, 'tm'), axis=0)]
where the time goes in v1:
time: 1260 us; the launch traced here: 1250 us
  waiting for transfers between devices  801 us (64%)
  other arithmetic  280 us (22%)
  blocking collectives  71.8 us (6%)
  starting transfers between devices  36 us (3%)
  local copies, waits for them, and re-layouts  22.2 us (2%)
  matrix products  19.5 us (2%)
  between operations  18.7 us (1%)
    all_gather x2, waiting for transfers between devices, shards(): gradient = jnp.sum(lax.all_gather(local_grad, 'tm'), axis=0)  771 us
    unnamed x1039, other arithmetic  239 us
    psum x4, blocking collectives, shards(): lax.psum(partial_value.astype(jnp.bfloat16), 'chan').astype(jnp.float32)  47.1 us
    ppermute x11, starting transfers between devices, shifted(): return lax.ppermute(shard, axis, pairs)  36 us
    ppermute x11, waiting for transfers between devices, shifted(): return lax.ppermute(shard, axis, pairs)  30.3 us
    reduce_sum x2, other arithmetic, shards(): gradient = jnp.sum(lax.all_gather(local_grad, 'tm'), axis=0)  26.3 us
  transfers between devices with their start and end apart: 13, of which 12 were waited for; matrix products, arithmetic and copies ran while one was open for 0% of the time, Pallas kernels for 0%

profile of v1, /device:TPU:1, one launch (start us, length us, event | category | flops | bytes accessed | tf_op | source)
XLA Modules:
  0.0 1249.7 jit_solution(3248532126996530965)
XLA Ops:
  7.2 5.0 copy.1215
  12.9 5.5 collective-permute-start
  18.4 3.6 copy.56
  87.9 3.6 constant_dynamic-update-slice_fusion.191
  92.9 4.7 collective-permute-done.1
  163.2 2.6 copy.58
  166.6 11.6 psum.70
  178.2 5.0 collective-permute-start.2
  188.6 5.1 collective-permute-done.3
  204.9 11.8 psum.71
  216.8 6.6 collective-permute-start.4
  231.1 3.6 collective-permute-done.5
  300.3 2.6 copy.69
  304.6 387.2 %all-gather.5.cloned.1.call-done = f32[1024,9216]{1,0:T(8,128)} async-done(((f32[16,9216]{1,0:T(8,128)}), f32[1024,9216]{1,0:T(8,128)}) %all-gather.5.cloned.1.call-update) | async-done | bytes 37748752 | tf_op jit(solution)/shard_map/all_gather | solution.py:77
  691.8 13.2 %reduce_sum.72 = f32[16,9216]{1,0:T(8,128)S(1)} reduce(f32[64,16,9216]{2,1,0:T(8,128)} %bitcast.4320, f32[]{:T(128)} %constant.26.clone.1), dimensions={0}, to_apply=%region_2.3 | reduce | flops 9289728 | bytes 38338564 | tf_op jit(solution)/shard_map/reduce_sum | solution.py:77
  706.2 6.4 all-reduce.1
  714.0 6.0 psum.74
  720.0 2.1 divide_dynamic-update-slice_fusion.1
  722.0 2.6 convert_element_type.92
  724.7 2.4 copy.70
  727.1 3.6 constant_dynamic-update-slice_fusion.671
  732.4 4.4 collective-permute-done.6
  748.1 11.4 psum.75
  759.6 4.2 collective-permute-start.7
  769.9 4.9 collective-permute-done.8
  786.1 12.3 psum.76
  798.5 6.0 collective-permute-start.9
  812.0 4.2 collective-permute-done.10
  828.9 383.5 %all-gather.7.cloned.1.call-done = f32[1024,9216]{1,0:T(8,128)} async-done(((f32[16,9216]{1,0:T(8,128)}), f32[1024,9216]{1,0:T(8,128)}) %all-gather.7.cloned.1.call-update) | async-done | bytes 37748752 | tf_op jit(solution)/shard_map/all_gather | solution.py:77
  1212.4 13.2 %reduce_sum.76 = f32[16,9216]{1,0:T(8,128)S(1)} reduce(f32[64,16,9216]{2,1,0:T(8,128)} %bitcast.4319, f32[]{:T(128)} %constant.26.clone.1), dimensions={0}, to_apply=%region_11.12 | reduce | flops 9289728 | bytes 38338564 | tf_op jit(solution)/shard_map/reduce_sum | solution.py:77
  1226.8 6.4 all-reduce
  1234.6 6.0 psum.79
  (1113 shorter events, 280.0 us)
Async XLA Ops:
  7.2 5.0 copy-start.4
  7.2 684.6 %all-gather.5.cloned.1.call-start = ((), (), s32[]{:S(2)}) async-start(), calls=%async_computation | async-start | bytes 38338560 | tf_op jit(solution)/shard_map/all_gather | solution.py:77
  12.9 9.1 collective-permute-start
  54.6 33.3 %copy-start.3 = (bf16[96,128]{1,0:T(8,128)(2,1)S(1)}, bf16[96,128]{1,0:T(8,128)(2,1)}, u32[]{:S(2)}) copy-start(bf16[96,128]{1,0:T(8,128)(2,1)} %param.5) | copy-start | bytes 73732
  87.9 5.0 copy-start.5
  91.5 6.1 collective-permute-start.1
  178.2 5.8 collective-permute-start.2
  187.3 6.4 collective-permute-start.3
  216.8 7.5 collective-permute-start.4
  226.7 1.6 copy-start.2
  226.7 3.1 copy-start.6
  228.3 6.3 collective-permute-start.5
  304.6 907.9 %all-gather.7.cloned.1.call-start = ((), (), s32[]{:S(2)}) async-start(), calls=%async_computation.1 | async-start | bytes 38338560 | tf_op jit(solution)/shard_map/all_gather | solution.py:77
  730.7 6.1 collective-permute-start.6
  759.6 5.1 collective-permute-start.7
  765.8 1.7 copy-start
  768.4 6.4 collective-permute-start.8
  798.5 7.0 collective-permute-start.9
  806.6 1.7 copy-start.1
  809.8 6.3 collective-permute-start.10
Sparse Core Ops, SparseCore 0:
  304.7 387.0 all-gather.4
  828.3 384.1 all-gather.6
